TPU v7x, 128 devices: a whole 4x4x4 slice. The times are simulated.
128 devices in a mesh: hours: 8 (over x_hi, z), sensor: 16 (over x_lo, y, core).
Axes of the slice: x: 4 (x_hi: 2, x_lo: 2; x = x_hi * 2 + x_lo), y: 4, z: 4, core: 2. Of those that a mesh axis runs over, the one named last changes fastest.
Arguments:
- coefficients: float32 [577, 16, 512], P(None, 'sensor'), may hold values from 5e-05 to 0.0053
- sky: float32 [577, 32768], P(None, ('hours', 'sensor')), may hold values from 0.1 to 10
- outdoor_air_warmth: float32 [32768], replicated, may hold values from -5 to 40
- hour_column: int32 [32768], replicated, may hold values from 0 to 32767, as said below
- module_of: int32 [16, 8, 64], P('sensor', 'hours'), may hold values from 0 to 7, as said below
Outputs:
- power: float32 [16, 8, 64, 32768], P('sensor', 'hours')
Inputs may be any that keep to these rules, and one draw needn't show every extreme that they name: `hour_column`: every column appears once, and the column of a time step lies in the same aligned run of 256 columns as the step itself. `module_of`: each module of a tracker row holds exactly 8 of the row's points.
All inputs are finite; a program needn't handle non-finite values.
Results may differ from a plain program's by a relative error of at most 0.0003.
Values sent between devices are 32-bit elements; how exact they have to be, the bound alone decides.
A program may use at most 128 MiB of HBM per device.

v0:
```python
import jax
import jax.numpy as jnp
from jax import lax
from jax.sharding import PartitionSpec as P

BLOCK_ROWS = 8
POINTS = 64
MODS = 8
WINDOW = 128


loss_multiplier = 0.0045
panel_warmup = 50.0
nominal_test_warmth = 25.0


def window_average(module_average):
    rows, mods, steps = module_average.shape
    shaped = module_average.reshape(rows, mods, steps // WINDOW, WINDOW)
    index = jnp.arange(WINDOW)
    upper = (index[:, None] <= index[None, :]).astype(jnp.float32)
    lower = (index[:, None] > index[None, :]).astype(jnp.float32)
    earlier = jnp.concatenate([jnp.zeros_like(shaped[:, :, :1]), shaped[:, :, :-1]], axis=2)
    within = jnp.einsum("rmbi,ij->rmbj", shaped, upper, precision=lax.Precision.HIGHEST)
    carried = jnp.einsum("rmbi,ij->rmbj", earlier, lower, precision=lax.Precision.HIGHEST)
    return (within + carried).reshape(rows, mods, steps) / WINDOW


def thermal_power(incident_flux, modules, outdoor_air_warmth):
    onehot = (modules[:, :, None] == jnp.arange(MODS, dtype=jnp.int32)[None, None, :]).astype(
        jnp.float32
    )
    module_average = jnp.einsum(
        "rqm,rqt->rmt", onehot, incident_flux, precision=lax.Precision.HIGHEST
    ) / (POINTS // MODS)
    heat = window_average(module_average)
    smoothing_span = jnp.einsum("rqm,rmt->rqt", onehot, heat, precision=lax.Precision.HIGHEST)
    junction_warmth = outdoor_air_warmth[None, None, :] + panel_warmup * smoothing_span
    return incident_flux * (1.0 - loss_multiplier * (junction_warmth - nominal_test_warmth))


def local_sky_order(sky, hour_column):
    width = sky.shape[1]
    owner = lax.axis_index("hours") * lax.axis_size("sensor") + lax.axis_index("sensor")
    first = owner * width
    own_steps = lax.dynamic_slice_in_dim(hour_column, first, width, 0)
    return jnp.take(sky, own_steps - first, axis=1)


def shards(coefficients, sky, outdoor_air_warmth, hour_column, module_of):
    contract_sensors = (((0,), (0,)), ((), ()))
    ordered_sky = local_sky_order(sky, hour_column)
    local_coeff = coefficients[:, 0, :]
    products = lax.dot_general(
        local_coeff,
        lax.all_gather(ordered_sky, "sensor", axis=1, tiled=True),
        contract_sensors,
        precision=lax.Precision.HIGHEST,
        preferred_element_type=jnp.float32,
    )
    products = products.reshape(BLOCK_ROWS, POINTS, products.shape[1])
    arrived = lax.all_to_all(products, "hours", split_axis=0, concat_axis=2, tiled=True)
    power = thermal_power(arrived, module_of[0], outdoor_air_warmth)
    return power[None]


def solution(mesh):
    return jax.shard_map(
        shards,
        mesh=mesh,
        in_specs=(
            P(None, "sensor", None),
            P(None, ("hours", "sensor")),
            P(),
            P(),
            P("sensor", "hours", None),
        ),
        out_specs=P("sensor", "hours", None, None),
        check_vma=False,
    )
```

profile of v0, /device:TPU:1, one launch (start us, length us, event | category | flops | bytes accessed | tf_op | source)
XLA Modules:
  0.0 219.4 jit_solution(13725217353478638661)
XLA Ops:
  6.5 0.0 copy-start
  6.5 0.0 all-gather.2.cloned.1.call-start
  6.5 0.9 compare_and_fusion
  7.4 1.3 copy.10
  8.7 1.1 gather_fusion
  9.8 0.9 select_bitcast_fusion
  10.8 0.0 all-gather.2.cloned.1.call-update
  10.8 65.8 %all-gather.2.cloned.1.call-done = f32[577,4096]{0,1:T(8,128)} async-done(((f32[577,256]{0,1:T(8,128)}), f32[577,4096]{0,1:T(8,128)}) %all-gather.2.cloned.1.call-update) | async-done | bytes 9453584 | tf_op jit(solution)/shard_map/all_gather | solution.py:56
  76.5 0.0 copy-done
  76.5 22.4 %fusion.8 = f32[4096,512]{0,1:T(8,128)S(1)} fusion(f32[577,4096]{0,1:T(8,128)} %all-gather.2.cloned.1.call-done, f32[577,1,512]{2,1,0:T(1,128)S(1)} %copy-done), kind=kOutput, calls=%fused_computation.12 | convolution fusion | flops 14520680448 | bytes 19023872 | tf_op jit(solution)/shard_map/dot_general | solution.py:54
  98.9 100.8 %all_to_all.18 = f32[8,64,4096]{2,1,0:T(8,128)S(1)} all-to-all(f32[8,64,4096]{2,1,0:T(8,128)S(1)} %bitcast.43), channel_id=1, replica_groups=mesh['hours'=8,'sensor'=16] {'hours'}, dimensions={0} | all-to-all | bytes 16777216 | tf_op jit(solution)/shard_map/all_to_all | solution.py:62
  199.7 0.0 copy-start.2
  199.7 1.0 copy.16
  200.7 0.0 copy-done.2
  200.7 0.0 copy-start.1
  200.7 2.8 %convolution_multiply_fusion.1 = f32[8,32768]{1,0:T(8,128)S(1)} fusion(f32[64,32768]{1,0:T(8,128)S(1)} %bitcast.41, s32[64]{0:T(128)S(1)} %bitcast.47), kind=kOutput, calls=%fused_computation.8 | convolution fusion | flops 201589248 | bytes 9437440 | tf_op jit(solution)/shard_map/rqm,rqt->rmt/dot_general | solution.py:33
  203.5 0.1 slice.6
  203.6 0.2 copy.15
  203.8 0.7 fusion.14
  204.5 0.7 fusion.7
  205.2 0.0 copy-done.1
  205.2 7.3 %fusion.5 = f32[1,1,64,32768]{3,2,1,0:T(8,128)} fusion(f32[64,32768]{1,0:T(8,128)S(1)} %bitcast.42, f32[32768]{0:T(1024)S(1)} %copy-done.1, f32[1,8,256,128]{3,2,1,0:T(8,128)S(1)} %fusion.7, s32[64]{0:T(128)S(1)} %bitcast.48), kind=kOutput, calls=%fused_computation.7 | convolution fusion | flops 213910016 | bytes 17957120 | tf_op jit(solution)/shard_map/rqm,rmt->rqt/dot_general | solution.py:37
  (1 shorter events, 0.0 us)
Async XLA Ops:
  6.5 70.0 %copy-start = (f32[577,1,512]{2,1,0:T(1,128)S(1)}, f32[577,1,512]{2,1,0:T(1,128)}, u32[]{:S(2)}) copy-start(f32[577,1,512]{2,1,0:T(1,128)} %param.5) | copy-start | bytes 3545092
  6.5 70.0 %all-gather.2.cloned.1.call-start = ((), (), s32[]{:S(2)}) async-start(), calls=%async_computation.1 | async-start | bytes 11141120 | tf_op jit(solution)/shard_map/all_gather | solution.py:56
  199.7 1.0 copy-start.2
  200.7 4.5 %copy-start.1 = (f32[32768]{0:T(1024)S(1)}, f32[32768]{0:T(1024)}, u32[]{:S(2)}) copy-start(f32[32768]{0:T(1024)} %param.7) | copy-start | bytes 393220
Sparse Core Ops, SparseCore 0:
  10.9 65.5 all-gather.1
where the time goes:
time: 220 us; the launch traced here: 219 us
  blocking collectives  101 us (46%)
  waiting for transfers between devices  65.8 us (30%)
  matrix products  33.9 us (15%)
  between operations  13.5 us (6%)
  local copies, waits for them, and re-layouts  3.66 us (2%)
    all_to_all x1, blocking collectives, shards(): lax.all_to_all(products, 'hours', split_axis=0, concat_axis=2, tiled=True)  101 us
    all_gather x1, waiting for transfers between devices, shards(): lax.all_gather(ordered_sky, 'sensor', axis=1, tiled=True)  65.8 us
    dot_general x1, matrix products, shards(): lax.dot_general(local_coeff, lax.all_gather(ordered_sky, 'sensor', axis=1...  22.4 us
    dot_general x1, matrix products, thermal_power(): jnp.einsum('rqm,rmt->rqt', onehot, heat, precision=lax.Precision.HIGHEST)  7.34 us
  transfers between devices with their start and end apart: 1, of which 1 were waited for; matrix products, arithmetic and copies ran while one was open for 0% of the time, Pallas kernels for 0%

commit v1 on v0

v1 whole, which is shorter than its diff:
```python
import functools

import jax
import jax.numpy as jnp
from jax import lax
from jax.experimental import pallas as pl
from jax.experimental.pallas import tpu as pltpu
from jax.sharding import PartitionSpec as P

MESH = pl.DeviceIdType.MESH
PATCHES = 577
ROWS = 584
DEPTH = 640
POINTS = 64
MODS = 8
WINDOW = 128
STEPS = 32768
WINDOWS = STEPS // WINDOW
SLOTS = 16

X, Y, Z = 0, 1, 2
PLANS = ((X, Y, Z, 480), (Z, Y, X, 416))

LOSS = 0.0045
WARMUP = 50.0
NOMINAL = 25.0


def coordinates():
    h, s = lax.axis_index("hours"), lax.axis_index("sensor")
    return (h // 4) * 2 + s // 8, (s // 2) % 4, h % 4, s % 2


def shifted(place, axis, by):
    moved = list(place)
    moved[axis] = (moved[axis] + by) % 4
    return tuple(moved)


def sibling(place):
    return place[0], place[1], place[2], 1 - place[3]


def device(place):
    x, y, z, c = place
    return (x // 2) * 4 + z, ((x % 2) * 4 + y) * 2 + c


def slot_of(i, j):
    return i * 4 + j


def middle(start, stop):
    return start + (stop - start) // 16 * 8


ORDER = (
    (3, 0), (1, 0), (0, 3), (0, 1), (2, 0), (0, 2), (3, 3), (1, 1), (3, 1), (1, 3),
    (2, 3), (2, 1), (3, 2), (1, 2), (2, 2),
)


def two_parts(value):
    high = value.astype(jnp.bfloat16)
    return high, (value - high.astype(jnp.float32)).astype(jnp.bfloat16)


def gather_kernel(
    coef_hbm, sky_hbm, hour_hbm, out_ref,
    coef_raw, sky_raw, hour_raw, coef_own, coef_sib, coef_x, coef_high, coef_low, sky_buf, sky_high, sky_low, prod,
    load_sem, sky_sems, sky_send, coef_sems, coef_send, prod_send, prod_recv,
):
    place = coordinates()
    x, y, z, c = place
    h, s = device(place)
    me = h * 16 + s
    loads = [
        pltpu.make_async_copy(sky_hbm, sky_raw, load_sem.at[0]),
        pltpu.make_async_copy(hour_hbm.at[pl.ds(pl.multiple_of((me // 4) * 8, 8), 8)], hour_raw, load_sem.at[1]),
        pltpu.make_async_copy(coef_hbm, coef_raw, load_sem.at[2]),
    ]
    for load in loads:
        load.start()

    partners = [sibling(place), shifted(place, Y, 1), shifted(place, Y, 3)]
    for axis in (X, Z):
        for k in (1, 2, 3):
            partners += [shifted(place, axis, k), sibling(shifted(place, axis, k))]
    barrier = pltpu.get_barrier_semaphore()
    for partner in partners:
        pl.semaphore_signal(barrier, inc=1, device_id=device(partner), device_id_type=MESH)

    loads[0].wait()
    loads[1].wait()
    sky_parts = two_parts(sky_raw[...])
    for half in range(2):
        column = hour_raw[pl.ds((me % 4) * 2 + half, 1), :] - me * 256
        chosen = (lax.broadcasted_iota(jnp.int32, (256, 128), 0) == column).astype(jnp.bfloat16)
        ordered = sum(jnp.dot(part, chosen, preferred_element_type=jnp.float32) for part in sky_parts)
        sky_buf[half, 0, pl.ds(PATCHES - 1, 8), :] = jnp.zeros((8, 128), jnp.float32)
        sky_buf[half, 0, pl.ds(0, PATCHES), :] = ordered
    sky_high[pl.ds(576, 64), :] = jnp.zeros((64, 128), jnp.bfloat16)
    sky_low[pl.ds(576, 64), :] = jnp.zeros((64, 128), jnp.bfloat16)
    pl.semaphore_wait(barrier, len(partners))

    def rows_of(half, part):
        cut = PLANS[half][3]
        return (0, cut) if part == 0 else (cut, ROWS)

    def send_sky(half, part, i, j, axis, by, which=None):
        start, stop = rows_of(half, part)
        if which == 0:
            stop = middle(start, stop)
        elif which == 1:
            start = middle(start, stop)
        first, second = PLANS[half][0], PLANS[half][1]
        to = slot_of((i - by) % 4, j) if axis == first else slot_of(i, (j - by) % 4)
        rows = pl.ds(start, stop - start)
        pltpu.make_async_remote_copy(
            src_ref=sky_buf.at[half, slot_of(i, j), rows],
            dst_ref=sky_buf.at[half, to, rows],
            send_sem=sky_send.at[half],
            recv_sem=sky_sems.at[half, part, to, which or 0],
            device_id=device(shifted(place, axis, by)),
            device_id_type=MESH,
        ).start()

    def await_sky(half, part, i, j):
        first, second = PLANS[half][:2] if part == 0 else PLANS[half][1::-1]
        along, across = (i, j) if part == 0 else (j, i)
        start, stop = rows_of(half, part)
        slot = slot_of(i, j)

        def wait(which, start, stop):
            rows = sky_buf.at[half, slot, pl.ds(start, stop - start)]
            pltpu.make_async_copy(rows, rows, sky_sems.at[half, part, slot, which]).wait()

        if across == 2 or (across == 0 and along == 2):
            wait(0, start, middle(start, stop))
            wait(1, middle(start, stop), stop)
        else:
            wait(0, start, stop)
        if across == 0:
            send_sky(half, part, i, j, second, 1)
            send_sky(half, part, i, j, second, -1)
            if along == 3:
                send_sky(half, part, i, j, first, 1, 0)
            if along == 1:
                send_sky(half, part, i, j, first, -1, 1)
        if across == 3:
            send_sky(half, part, i, j, second, 1, 0)
        if across == 1:
            send_sky(half, part, i, j, second, -1, 1)

    for half in range(2):
        for part in range(2):
            for axis in PLANS[half][:2]:
                send_sky(half, part, 0, 0, axis, 1)
                send_sky(half, part, 0, 0, axis, -1)

    loads[2].wait()
    coef_own[:, pl.ds(512, 128)] = jnp.zeros((512, 128), jnp.float32)
    for tile in range(4):
        lanes = pl.ds(tile * 128, 128)
        whole = coef_raw[:, 0, lanes]
        coef_own[lanes, pl.ds(0, PATCHES)] = whole.T

    def coef_copy(src, dst, sem, to):
        return pltpu.make_async_remote_copy(
            src_ref=src, dst_ref=dst, send_sem=coef_send.at[sem], recv_sem=coef_sems.at[sem],
            device_id=device(to), device_id_type=MESH,
        )

    own_row = coef_own.at[pl.ds(pl.multiple_of(h * 64, 64), 64)]
    to_next = coef_copy(own_row, coef_x.at[1, 0], 1, shifted(place, X, 1))
    to_last = coef_copy(own_row, coef_x.at[0, 0], 2, shifted(place, X, 3))
    to_sibling = coef_copy(coef_own, coef_sib, 0, sibling(place))
    to_next.start()
    to_last.start()
    to_sibling.start()

    def put_coef(half, k, other, value):
        high, low = two_parts(value)
        rows = pl.ds((k * 2 + other) * 64, 64)
        coef_high[half, rows, :] = high
        coef_low[half, rows, :] = low

    def row_at(half, k):
        at = (x // 2) * 4 + (z + k) % 4 if half == 0 else (((x + k) % 4) // 2) * 4 + z
        return pl.ds(pl.multiple_of(at * 64, 64), 64)

    for k in range(4):
        put_coef(0, k, 0, coef_own[row_at(0, k), :])
    for k in (0, 2):
        put_coef(1, k, 0, coef_own[row_at(1, k), :])
    to_sibling.wait()
    for k in range(4):
        put_coef(0, k, 1, coef_sib[row_at(0, k), :])
    for k in (0, 2):
        put_coef(1, k, 1, coef_sib[row_at(1, k), :])

    def multiply(half, i, j):
        slot = slot_of(i, j)
        axis = PLANS[half][2]
        high, low = two_parts(sky_buf[half, slot, pl.ds(0, 576), :])
        sky_high[pl.ds(0, 576), :] = high
        sky_low[pl.ds(0, 576), :] = low
        high, low = two_parts(sky_buf[half, slot, pl.ds(576, 8), :])
        pad = jnp.zeros((8, 128), jnp.bfloat16)
        sky_high[pl.ds(576, 16), :] = jnp.concatenate([high, pad], axis=0)
        sky_low[pl.ds(576, 16), :] = jnp.concatenate([low, pad], axis=0)

        @pl.loop(0, 2)
        def _(tile):
            rows = pl.ds(pl.multiple_of(tile * 256, 256), 256)
            prod[half, slot, rows, :] = (
                jnp.dot(coef_high[half, rows, :], sky_low[...], preferred_element_type=jnp.float32)
                + jnp.dot(coef_low[half, rows, :], sky_high[...], preferred_element_type=jnp.float32)
            ) + jnp.dot(coef_high[half, rows, :], sky_high[...], preferred_element_type=jnp.float32)

        oh, os = device(shifted(shifted(place, PLANS[half][0], i), PLANS[half][1], j))
        window = (oh * 16 + os) * 2 + half
        out_ref[window] = prod[half, slot, pl.ds(0, 64), :]
        for k in (2, 1, 3, 0):
            for other in range(2):
                if (k, other) == (0, 0):
                    continue
                to = shifted(place, axis, k)
                pltpu.make_async_remote_copy(
                    src_ref=prod.at[half, slot, pl.ds((k * 2 + other) * 64, 64)],
                    dst_ref=out_ref.at[window],
                    send_sem=prod_send.at[half],
                    recv_sem=prod_recv,
                    device_id=device(sibling(to) if other else to),
                    device_id_type=MESH,
                ).start()

    multiply(0, 0, 0)
    to_next.wait()
    to_last.wait()
    on = [coef_copy(coef_x.at[n, 0], coef_x.at[n, 1], 3 + n, sibling(place)) for n in range(2)]
    for copy in on:
        copy.start()
    for half in range(2):
        for i, j in ORDER[:4]:
            await_sky(half, 0, i, j)
            await_sky(half, 1, i, j)
    for n, k in enumerate((1, 3)):
        put_coef(1, k, 0, coef_x[n, 0])
    for n, k in enumerate((1, 3)):
        on[n].wait()
        put_coef(1, k, 1, coef_x[n, 1])
    multiply(1, 0, 0)
    for n, (i, j) in enumerate(ORDER):
        for half in range(2):
            if n >= 4:
                await_sky(half, 0, i, j)
                await_sky(half, 1, i, j)
            multiply(half, i, j)

    for half in range(2):
        sent = sky_buf.at[half, pl.ds(0, 15)]
        pltpu.make_async_copy(sent, sent, sky_send.at[half]).wait()
        sent = prod.at[half, pl.ds(0, 14)]
        pltpu.make_async_copy(sent, sent, prod_send.at[half]).wait()
    came = out_ref.at[pl.ds(0, WINDOWS // 8 * 7)]
    pltpu.make_async_copy(came, came, prod_recv).wait()


def irradiance(coefficients, sky, hours):
    f32, bf16 = jnp.float32, jnp.bfloat16
    vmem, dma = pltpu.VMEM, pltpu.SemaphoreType.DMA
    return pl.pallas_call(
        gather_kernel,
        out_shape=jax.ShapeDtypeStruct((WINDOWS, POINTS, WINDOW), f32),
        in_specs=[pl.BlockSpec(memory_space=pl.ANY)] * 3,
        out_specs=pl.BlockSpec(memory_space=pltpu.VMEM),
        scratch_shapes=[
            vmem((PATCHES, 1, 512), f32),
            vmem((PATCHES, 256), f32),
            vmem((8, 128), jnp.int32),
            vmem((512, DEPTH), f32),
            vmem((512, DEPTH), f32),
            vmem((2, 2, 64, DEPTH), f32),
            vmem((2, 512, DEPTH), bf16),
            vmem((2, 512, DEPTH), bf16),
            vmem((2, SLOTS, ROWS, 128), f32),
            vmem((DEPTH, 128), bf16),
            vmem((DEPTH, 128), bf16),
            vmem((2, SLOTS, 512, 128), f32),
            dma((3,)),
            dma((2, 2, SLOTS, 2)),
            dma((2,)),
            dma((5,)),
            dma((5,)),
            dma((2,)),
            dma,
        ],
        compiler_params=pltpu.CompilerParams(
            collective_id=0, has_side_effects=True, vmem_limit_bytes=56 << 20
        ),
        name="irradiance",
    )(coefficients, sky, hours)


GROUP = 16


def thermal_kernel(flux_ref, air_ref, module_ref, out_ref, means, factor):
    f32, bf16 = jnp.float32, jnp.bfloat16

    @pl.when(pl.program_id(0) == 0)
    def _():
        means[pl.ds(0, MODS), :] = jnp.zeros((MODS, WINDOW), f32)

    @pl.when(pl.program_id(0) > 0)
    def _():
        means[pl.ds(0, MODS), :] = means[pl.ds(GROUP * MODS, MODS), :]

    member = lax.broadcasted_iota(jnp.int32, (MODS, POINTS), 0) == module_ref[...]
    onehot = member.astype(bf16)
    both = jnp.concatenate([onehot, onehot], axis=1)
    for w in range(GROUP):
        stacked = jnp.concatenate(two_parts(flux_ref[w]), axis=0)
        mean = jnp.dot(both, stacked, preferred_element_type=f32) / (POINTS // MODS)
        means[pl.ds((w + 1) * MODS, MODS), :] = mean
    row = lax.broadcasted_iota(jnp.int32, (WINDOW, WINDOW), 0)
    col = lax.broadcasted_iota(jnp.int32, (WINDOW, WINDOW), 1)
    upper, lower = (row <= col).astype(bf16), (row > col).astype(bf16)
    heat = jnp.zeros((GROUP * MODS, WINDOW), f32)
    for first, weights in ((MODS, upper), (0, lower)):
        for part in two_parts(means[pl.ds(first, GROUP * MODS), :]):
            heat = heat + jnp.dot(part, weights, preferred_element_type=f32)
    heat = heat / WINDOW
    name = lax.broadcasted_iota(jnp.int32, (MODS, WINDOW), 0).astype(bf16)
    index = lax.dot_general(onehot, name, (((0,), (0,)), ((), ())), preferred_element_type=f32)
    index = index.astype(jnp.int32)
    for w in range(GROUP):
        warmth = air_ref[pl.ds(w, 1), :] + WARMUP * heat[w * MODS : (w + 1) * MODS, :]
        scale = 1.0 - LOSS * (warmth - NOMINAL)
        for r in range(POINTS // 8):
            spread = jnp.take_along_axis(scale, index[r * 8 : (r + 1) * 8, :], axis=0)
            rows = pl.ds(r * 8, 8)
            out_ref[rows, pl.ds(w * WINDOW, WINDOW)] = flux_ref[w, rows, :] * spread


def thermal_power(flux, air, modules):
    return pl.pallas_call(
        thermal_kernel,
        grid=(WINDOWS // GROUP,),
        out_shape=jax.ShapeDtypeStruct((POINTS, STEPS), jnp.float32),
        in_specs=[
            pl.BlockSpec((GROUP, POINTS, WINDOW), lambda g: (g, 0, 0)),
            pl.BlockSpec((GROUP, WINDOW), lambda g: (g, 0)),
            pl.BlockSpec((1, POINTS), lambda g: (0, 0)),
        ],
        out_specs=pl.BlockSpec((POINTS, GROUP * WINDOW), lambda g: (0, g)),
        scratch_shapes=[
            pltpu.VMEM(((GROUP + 1) * MODS, WINDOW), jnp.float32),
            pltpu.VMEM((8, WINDOW), jnp.float32),
        ],
        name="thermal",
    )(flux, air, modules)


def shards(coefficients, sky, outdoor_air_warmth, hour_column, module_of):
    flux = irradiance(coefficients, sky, hour_column.reshape(WINDOWS, WINDOW))
    power = thermal_power(flux, outdoor_air_warmth.reshape(WINDOWS, WINDOW), module_of.reshape(1, POINTS))
    return power.reshape(1, 1, POINTS, STEPS)


def solution(mesh):
    return jax.shard_map(
        shards,
        mesh=mesh,
        in_specs=(
            P(None, "sensor", None),
            P(None, ("hours", "sensor")),
            P(),
            P(),
            P("sensor", "hours", None),
        ),
        out_specs=P("sensor", "hours", None, None),
        check_vma=False,
    )
```

time: 220 us -> 106 us (0.48)
  Pallas kernels: 0 us -> 105 us
  blocking collectives: 101 us -> 0 us
  waiting for transfers between devices: 65.8 us -> 0 us
  matrix products: 33.9 us -> 0 us
  between operations: 13.5 us -> 0.01 us
  local copies, waits for them, and re-layouts: 3.66 us -> 0 us
    pallas_call x0 -> x2, Pallas kernels: none -> 105 us  [the longest x1 89.3 us: irradiance(): pl.pallas_call(gather_kernel, out_shape=jax.ShapeDtypeStruct((WINDOWS, PO...]
    all_to_all x1 -> x0, blocking collectives: 101 us -> none  [shards(): lax.all_to_all(products, 'hours', split_axis=0, concat_axis=2, tiled=True)]
    all_gather x1 -> x0, waiting for transfers between devices: 65.8 us -> none  [shards(): lax.all_gather(ordered_sky, 'sensor', axis=1, tiled=True)]
    dot_general x5 -> x0, matrix products: 33.9 us -> none  [the longest x1 22.4 us: shards(): lax.dot_general(local_coeff, lax.all_gather(ordered_sky, 'sensor', axis=1...]
    unnamed x9 -> x0, local copies, waits for them, and re-layouts: 2.5 us -> none
  transfers between devices with their start and end apart: 1 -> 0, of which waited for: 1 -> 0; matrix products, arithmetic and copies ran while one was open for 0% -> 0% of each run, Pallas kernels for 0% -> 0%
where the time goes in v1:
time: 106 us; the launch traced here: 105 us
  Pallas kernels  105 us (99%)
    pallas_call x1, Pallas kernels, irradiance(): pl.pallas_call(gather_kernel, out_shape=jax.ShapeDtypeStruct((WINDOWS, PO...  89.3 us
    pallas_call x1, Pallas kernels, thermal_power(): pl.pallas_call(thermal_kernel, grid=(WINDOWS // GROUP,), out_shape=jax.Sh...  15.9 us

profile of v1, /device:TPU:1, one launch (start us, length us, event | category | flops | bytes accessed | tf_op | source)
XLA Modules:
  0.0 105.1 jit_solution(18195273948077025078)
XLA Ops:
  0.0 89.3 %irradiance.1.flux_ref = f32[256,64,128]{2,1,0:T(8,128)} custom-call(f32[577,1,512]{2,1,0:T(1,128)} %coef_hbm.1, f32[577,256]{1,0:T(8,128)} %sky_hbm.1, s32[256,128]{1,0:T(8,128)} %bitcast.4), custom_call_target="tpu_custom_call" | custom-call | tf_op jit(solution)/shard_map/irradiance/pallas_call | solution.py:273
  89.3 15.9 %thermal.1 = f32[64,32768]{1,0:T(8,128)} custom-call(f32[256,64,128]{2,1,0:T(8,128)} %irradiance.1.flux_ref, f32[256,128]{1,0:T(8,128)} %bitcast.5, s32[1,64]{1,0:T(1,128)} %bitcast.6), custom_call_target="tpu_custom_call" | custom-call | tf_op jit(solution)/shard_map/thermal/pallas_call | solution.py:348

commit v2 on v1

v2 whole, which is shorter than its diff:
```python
import functools

import jax
import jax.numpy as jnp
from jax import lax
from jax.experimental import pallas as pl
from jax.experimental.pallas import tpu as pltpu
from jax.sharding import PartitionSpec as P

MESH = pl.DeviceIdType.MESH
PATCHES = 577
ROWS = 584
DEPTH = 640
POINTS = 64
MODS = 8
WINDOW = 128
STEPS = 32768
WINDOWS = STEPS // WINDOW
SLOTS = 16

CUT = 408
VLIM = 32 << 20

LOSS = 0.0045
WARMUP = 50.0
NOMINAL = 25.0


def coordinates():
    h, s = lax.axis_index("hours"), lax.axis_index("sensor")
    return (h // 4) * 2 + s // 8, (s // 2) % 4, h % 4, s % 2


def along_first(place, by):
    x, y, z, c = place
    return (x + by * (1 - c)) % 4, y, (z + by * c) % 4, c


def along_second(place, by):
    x, y, z, c = place
    return x, (y + by) % 4, z, c


def along_third(place, by):
    x, y, z, c = place
    return (x + by * c) % 4, y, (z + by * (1 - c)) % 4, c


def along_x(place, by):
    x, y, z, c = place
    return (x + by) % 4, y, z, c


def sibling(place):
    x, y, z, c = place
    return x, y, z, 1 - c


def device(place):
    x, y, z, c = place
    return (x // 2) * 4 + z, ((x % 2) * 4 + y) * 2 + c


def slot_of(i, j):
    return i * 4 + j


def middle(start, stop):
    return start + (stop - start) // 16 * 8


def two_parts(value):
    high = value.astype(jnp.bfloat16)
    return high, (value - high.astype(jnp.float32)).astype(jnp.bfloat16)


def gather_kernel(
    coef_hbm, sky_hbm, hour_hbm, out_ref,
    coef_raw, sky_raw, hour_raw, coef_own, coef_sib, coef_x, coef_high, coef_low, sky_buf, sky_high, sky_low, prod,
    load_sem, sky_sems, sky_send, coef_sems, coef_send, prod_send, prod_recv, prod_own,
):
    place = coordinates()
    x, y, z, c = place
    h, s = device(place)
    me = h * 16 + s
    loads = [
        pltpu.make_async_copy(sky_hbm, sky_raw, load_sem.at[0]),
        pltpu.make_async_copy(hour_hbm.at[pl.ds(pl.multiple_of((me // 4) * 8, 8), 8)], hour_raw, load_sem.at[1]),
        pltpu.make_async_copy(coef_hbm, coef_raw, load_sem.at[2]),
    ]
    for load in loads:
        load.start()

    partners = [along_second(place, 1), along_second(place, 3), sibling(place)]
    for k in (1, 2, 3):
        for partner in (along_third(place, k), along_first(place, k)):
            partners += [partner, sibling(partner)]
    barrier = pltpu.get_barrier_semaphore()
    for partner in partners:
        pl.semaphore_signal(barrier, inc=1, device_id=device(partner), device_id_type=MESH)

    loads[0].wait()
    loads[1].wait()
    sky_parts = two_parts(sky_raw[...])
    sky_buf[0, pl.ds(PATCHES - 1, 8), :] = jnp.zeros((8, 256), jnp.float32)
    for half in range(2):
        column = hour_raw[pl.ds((me % 4) * 2 + half, 1), :] - me * 256
        chosen = (lax.broadcasted_iota(jnp.int32, (256, 128), 0) == column).astype(jnp.bfloat16)
        ordered = sum(jnp.dot(part, chosen, preferred_element_type=jnp.float32) for part in sky_parts)
        sky_buf[0, pl.ds(0, PATCHES), pl.ds(half * 128, 128)] = ordered
    sky_high[pl.ds(576, 64), :] = jnp.zeros((64, 256), jnp.bfloat16)
    sky_low[pl.ds(576, 64), :] = jnp.zeros((64, 256), jnp.bfloat16)
    pl.semaphore_wait(barrier, len(partners))

    rows_of = ((0, CUT), (CUT, ROWS))

    def send_sky(part, i, j, second, by, which=None):
        start, stop = rows_of[part]
        if which == 0:
            stop = middle(start, stop)
        elif which == 1:
            start = middle(start, stop)
        to = slot_of(i, (j - by) % 4) if second else slot_of((i - by) % 4, j)
        rows = pl.ds(start, stop - start)
        pltpu.make_async_remote_copy(
            src_ref=sky_buf.at[slot_of(i, j), rows],
            dst_ref=sky_buf.at[to, rows],
            send_sem=sky_send,
            recv_sem=sky_sems.at[part, to, which or 0],
            device_id=device((along_second if second else along_first)(place, by % 4)),
            device_id_type=MESH,
        ).start()

    def await_sky(part, i, j):
        along, across = (i, j) if part == 0 else (j, i)
        start, stop = rows_of[part]
        slot = slot_of(i, j)

        def wait(which, start, stop):
            rows = sky_buf.at[slot, pl.ds(start, stop - start)]
            pltpu.make_async_copy(rows, rows, sky_sems.at[part, slot, which]).wait()

        if across == 2 or (across == 0 and along == 2):
            wait(0, start, middle(start, stop))
            wait(1, middle(start, stop), stop)
        elif (part, i) == (0, 0):
            wait(0, start, middle(start, stop))
            wait(1, middle(start, stop), stop)
        else:
            wait(0, start, stop)
        inner, outer = part == 1, part == 0
        if across == 0:
            if along == 3:
                send_sky(part, i, j, inner, 1, 0)
            if along == 1:
                send_sky(part, i, j, inner, -1, 1)
            send_sky(part, i, j, outer, 1)
            send_sky(part, i, j, outer, -1)
        if across == 3:
            send_sky(part, i, j, outer, 1, 0)
        if across == 1:
            send_sky(part, i, j, outer, -1, 1)

    for part, second, which in ((0, False, None), (1, True, None), (0, True, 0), (1, False, None)):
        send_sky(part, 0, 0, second, 1, which)
        send_sky(part, 0, 0, second, -1, which)

    loads[2].wait()
    coef_own[:, pl.ds(512, 128)] = jnp.zeros((512, 128), jnp.float32)
    for tile in range(4):
        lanes = pl.ds(tile * 128, 128)
        whole = coef_raw[:, 0, lanes]
        coef_own[lanes, pl.ds(0, PATCHES)] = whole.T

    def coef_copy(src, dst, sem, to):
        return pltpu.make_async_remote_copy(
            src_ref=src, dst_ref=dst, send_sem=coef_send.at[sem], recv_sem=coef_sems.at[sem],
            device_id=device(to), device_id_type=MESH,
        )

    def row_of(place):
        return pl.ds(pl.multiple_of(device(place)[0] * 64, 64), 64)

    def put_coef(k, other, value):
        high, low = two_parts(value)
        rows = pl.ds((k * 2 + other) * 64, 64)
        coef_high[rows, :] = high
        coef_low[rows, :] = low

    def x_copies(source, other):
        return [
            coef_copy(source.at[row_of(place)], coef_x.at[n, other], 1 + n * 2 + other, along_x(place, by))
            for n, by in ((0, 3), (1, 1))
        ]

    to_sibling = coef_copy(coef_own, coef_sib, 0, sibling(place))
    to_sibling.start()

    @pl.when(c == 1)
    def _():
        for copy in x_copies(coef_own, 0):
            copy.start()

    for k in (0, 2):
        put_coef(k, 0, coef_own[row_of(along_third(place, k)), :])

    @pl.when(c == 0)
    def _():
        for k in (1, 3):
            put_coef(k, 0, coef_own[row_of(along_third(place, k)), :])

    to_sibling.wait()

    @pl.when(c == 1)
    def _():
        for copy in x_copies(coef_sib, 1):
            copy.start()

    for k in (0, 2):
        put_coef(k, 1, coef_sib[row_of(along_third(place, k)), :])

    @pl.when(c == 0)
    def _():
        for k in (1, 3):
            put_coef(k, 1, coef_sib[row_of(along_third(place, k)), :])

    def await_all(*parts):
        for part, i, j in parts:
            await_sky(part, i, j)

    await_all((1, 0, 3), (1, 0, 1))
    send_sky(0, 0, 0, True, 1, 1)
    send_sky(0, 0, 0, True, -1, 1)
    await_all((0, 3, 0), (0, 1, 0), (1, 3, 0), (1, 1, 0))

    @pl.when(c == 1)
    def _():
        for other in range(2):
            for n, copy in enumerate(x_copies((coef_own, coef_sib)[other], other)):
                copy.wait()
                put_coef(2 * n + 1, other, coef_x[n, other])

    def multiply(i, j):
        slot = slot_of(i, j)
        high, low = two_parts(sky_buf[slot, pl.ds(0, 576), :])
        sky_high[pl.ds(0, 576), :] = high
        sky_low[pl.ds(0, 576), :] = low
        high, low = two_parts(sky_buf[slot, pl.ds(576, 8), :])
        pad = jnp.zeros((8, 256), jnp.bfloat16)
        sky_high[pl.ds(576, 16), :] = jnp.concatenate([high, pad], axis=0)
        sky_low[pl.ds(576, 16), :] = jnp.concatenate([low, pad], axis=0)

        @pl.loop(0, 2)
        def _(tile):
            rows = pl.ds(pl.multiple_of(tile * 256, 256), 256)
            both = (
                jnp.dot(coef_high[rows, :], sky_low[...], preferred_element_type=jnp.float32)
                + jnp.dot(coef_low[rows, :], sky_high[...], preferred_element_type=jnp.float32)
            ) + jnp.dot(coef_high[rows, :], sky_high[...], preferred_element_type=jnp.float32)
            for half in range(2):
                prod[slot, half, rows, :] = both[:, half * 128 : (half + 1) * 128]

        owner_h, owner_s = device(along_second(along_first(place, i), j))
        windows = pl.ds((owner_h * 16 + owner_s) * 2, 2)
        for k in (2, 1, 3, 0):
            for other in range(2):
                source = prod.at[slot, :, pl.ds((k * 2 + other) * 64, 64)]
                if (k, other) == (0, 0):
                    pltpu.make_async_copy(source, out_ref.at[windows], prod_own).start()
                    continue
                to = along_third(place, k)
                pltpu.make_async_remote_copy(
                    src_ref=source,
                    dst_ref=out_ref.at[windows],
                    send_sem=prod_send,
                    recv_sem=prod_recv,
                    device_id=device(sibling(to) if other else to),
                    device_id_type=MESH,
                ).start()

    def multiply_all(*chunks):
        for i, j in chunks:
            multiply(i, j)

    multiply_all((0, 0), (3, 0), (1, 0))
    await_all((1, 0, 2), (1, 3, 3), (1, 3, 1), (1, 1, 3), (1, 1, 1), (0, 2, 0), (1, 2, 0))
    multiply_all((2, 0))
    await_all((0, 0, 3), (0, 0, 1))
    multiply_all((0, 3), (0, 1))
    await_all((1, 3, 2), (1, 1, 2))
    await_all((0, 3, 3), (0, 3, 1))
    multiply_all((3, 3), (3, 1))
    await_all((0, 1, 3), (0, 1, 1))
    multiply_all((1, 3), (1, 1))
    await_all((1, 2, 3), (1, 2, 1), (1, 2, 2), (0, 2, 3), (0, 2, 1))
    multiply_all((2, 3), (2, 1))
    for i in (0, 3, 1, 2):
        await_all((0, i, 2))
        multiply_all((i, 2))

    def finish(ref, sem):
        pltpu.make_async_copy(ref, ref, sem).wait()

    finish(sky_buf.at[pl.ds(0, 15)], sky_send)
    finish(prod.at[pl.ds(0, 14)], prod_send)
    finish(prod.at[pl.ds(0, 2)], prod_own)
    finish(out_ref.at[pl.ds(0, WINDOWS // 8 * 7)], prod_recv)

def irradiance(coefficients, sky, hours):
    coefficients, sky, hours = [pltpu.with_memory_space_constraint(a, pltpu.HBM) for a in (coefficients, sky, hours)]
    f32, bf16 = jnp.float32, jnp.bfloat16
    vmem, dma = pltpu.VMEM, pltpu.SemaphoreType.DMA
    return pl.pallas_call(
        gather_kernel,
        out_shape=jax.ShapeDtypeStruct((WINDOWS, POINTS, WINDOW), f32),
        in_specs=[pl.BlockSpec(memory_space=pltpu.HBM)] * 3,
        out_specs=pl.BlockSpec(memory_space=pl.ANY),
        scratch_shapes=[
            vmem((PATCHES, 1, 512), f32),
            vmem((PATCHES, 256), f32),
            vmem((8, 128), jnp.int32),
            vmem((512, DEPTH), f32),
            vmem((512, DEPTH), f32),
            vmem((2, 2, 64, DEPTH), f32),
            vmem((512, DEPTH), bf16),
            vmem((512, DEPTH), bf16),
            vmem((SLOTS, ROWS, 256), f32),
            vmem((DEPTH, 256), bf16),
            vmem((DEPTH, 256), bf16),
            vmem((SLOTS, 2, 512, 128), f32),
            dma((3,)),
            dma((2, SLOTS, 2)),
            dma,
            dma((5,)),
            dma((5,)),
            dma,
            dma,
            dma,
        ],
        compiler_params=pltpu.CompilerParams(
            collective_id=0, has_side_effects=True, vmem_limit_bytes=VLIM
        ),
        name="irradiance",
    )(coefficients, sky, hours)


GROUP = 64


def thermal_kernel(flux_ref, air_ref, module_ref, out_ref, means):
    f32, bf16 = jnp.float32, jnp.bfloat16

    @pl.when(pl.program_id(0) == 0)
    def _():
        means[pl.ds(0, MODS), :] = jnp.zeros((MODS, WINDOW), f32)

    @pl.when(pl.program_id(0) > 0)
    def _():
        means[pl.ds(0, MODS), :] = means[pl.ds(GROUP * MODS, MODS), :]

    member = lax.broadcasted_iota(jnp.int32, (MODS, POINTS), 0) == module_ref[...]
    onehot = member.astype(bf16)
    both = jnp.concatenate([onehot, onehot], axis=1)
    for w in range(GROUP):
        stacked = jnp.concatenate(two_parts(flux_ref[w]), axis=0)
        mean = jnp.dot(both, stacked, preferred_element_type=f32) / (POINTS // MODS)
        means[pl.ds((w + 1) * MODS, MODS), :] = mean
    row = lax.broadcasted_iota(jnp.int32, (WINDOW, WINDOW), 0)
    col = lax.broadcasted_iota(jnp.int32, (WINDOW, WINDOW), 1)
    upper, lower = (row <= col).astype(bf16), (row > col).astype(bf16)
    heat = jnp.zeros((GROUP * MODS, WINDOW), f32)
    for first, weights in ((MODS, upper), (0, lower)):
        for part in two_parts(means[pl.ds(first, GROUP * MODS), :]):
            heat = heat + jnp.dot(part, weights, preferred_element_type=f32)
    heat = heat / WINDOW
    name = lax.broadcasted_iota(jnp.int32, (MODS, WINDOW), 0).astype(bf16)
    index = lax.dot_general(onehot, name, (((0,), (0,)), ((), ())), preferred_element_type=f32)
    index = index.astype(jnp.int32)
    for w in range(GROUP):
        warmth = air_ref[pl.ds(w, 1), :] + WARMUP * heat[w * MODS : (w + 1) * MODS, :]
        scale = 1.0 - LOSS * (warmth - NOMINAL)
        for r in range(POINTS // 8):
            spread = jnp.take_along_axis(scale, index[r * 8 : (r + 1) * 8, :], axis=0)
            rows = pl.ds(r * 8, 8)
            out_ref[rows, pl.ds(w * WINDOW, WINDOW)] = flux_ref[w, rows, :] * spread


def thermal_power(flux, air, modules):
    return pl.pallas_call(
        thermal_kernel,
        grid=(WINDOWS // GROUP,),
        out_shape=jax.ShapeDtypeStruct((POINTS, STEPS), jnp.float32),
        in_specs=[
            pl.BlockSpec((GROUP, POINTS, WINDOW), lambda g: (g, 0, 0)),
            pl.BlockSpec((GROUP, WINDOW), lambda g: (g, 0)),
            pl.BlockSpec((1, POINTS), lambda g: (0, 0)),
        ],
        out_specs=pl.BlockSpec((POINTS, GROUP * WINDOW), lambda g: (0, g)),
        scratch_shapes=[
            pltpu.VMEM(((GROUP + 1) * MODS, WINDOW), jnp.float32),
        ],
        compiler_params=pltpu.CompilerParams(vmem_limit_bytes=16 << 20),
        name="thermal",
    )(flux, air, modules)


def shards(coefficients, sky, outdoor_air_warmth, hour_column, module_of):
    flux = irradiance(coefficients, sky, hour_column.reshape(WINDOWS, WINDOW))
    power = thermal_power(flux, outdoor_air_warmth.reshape(WINDOWS, WINDOW), module_of.reshape(1, POINTS))
    return power.reshape(1, 1, POINTS, STEPS)


def solution(mesh):
    return jax.shard_map(
        shards,
        mesh=mesh,
        in_specs=(
            P(None, "sensor", None),
            P(None, ("hours", "sensor")),
            P(),
            P(),
            P("sensor", "hours", None),
        ),
        out_specs=P("sensor", "hours", None, None),
        check_vma=False,
    )
```

time: 106 us -> 86.1 us (0.81)
  Pallas kernels: 105 us -> 85.9 us
    pallas_call x1, Pallas kernels: 89.3 us -> 79.5 us  [irradiance(): pl.pallas_call(gather_kernel, out_shape=jax.ShapeDtypeStruct((WINDOWS, PO...]
    pallas_call x1, Pallas kernels: 15.9 us -> 6.44 us  [thermal_power(): pl.pallas_call(thermal_kernel, grid=(WINDOWS // GROUP,), out_shape=jax.Sh...]
where the time goes in v2:
time: 86.1 us; the launch traced here: 86 us
  Pallas kernels  85.9 us (100%)
    pallas_call x1, Pallas kernels, irradiance(): pl.pallas_call(gather_kernel, out_shape=jax.ShapeDtypeStruct((WINDOWS, PO...  79.5 us
    pallas_call x1, Pallas kernels, thermal_power(): pl.pallas_call(thermal_kernel, grid=(WINDOWS // GROUP,), out_shape=jax.Sh...  6.44 us

profile of v2, /device:TPU:1, one launch (start us, length us, event | category | flops | bytes accessed | tf_op | source)
XLA Modules:
  0.0 86.0 jit_solution(9271104341363999447)
XLA Ops:
  0.0 0.0 copy-start.1
  0.0 0.0 copy-start
  0.0 79.5 %irradiance.1.flux_ref = f32[256,64,128]{2,1,0:T(8,128)S(1)} custom-call(f32[577,1,512]{2,1,0:T(1,128)} %coef_hbm.1, f32[577,256]{1,0:T(8,128)} %sky_hbm.1, s32[256,128]{1,0:T(8,128)} %bitcast.6), custom_call_target="tpu_custom_call" | custom-call | tf_op jit(solution)/shard_map/irradiance/pallas_call | solution.py:313
  79.5 0.0 copy-done.1
  79.5 0.0 copy-done
  79.5 6.4 %thermal.1 = f32[64,32768]{1,0:T(8,128)} custom-call(f32[256,64,128]{2,1,0:T(8,128)S(1)} %irradiance.1.flux_ref, f32[256,128]{1,0:T(8,128)S(1)} %bitcast.4, s32[1,64]{1,0:T(1,128)S(1)} %bitcast.5), custom_call_target="tpu_custom_call" | custom-call | tf_op jit(solution)/shard_map/thermal/pallas_call | solution.py:389
Async XLA Ops:
  0.0 79.5 %copy-start.1 = (s32[1,1,64]{2,1,0:T(1,128)S(1)}, s32[1,1,64]{2,1,0:T(1,128)}, u32[]{:S(2)}) copy-start(s32[1,1,64]{2,1,0:T(1,128)} %param.9) | copy-start | bytes 772
  0.0 79.5 %copy-start = (f32[32768]{0:T(1024)S(1)}, f32[32768]{0:T(1024)}, u32[]{:S(2)}) copy-start(f32[32768]{0:T(1024)} %param.7) | copy-start | bytes 393220

commit v3 on v2

--- a/solution.py
+++ b/solution.py
@@ -18,8 +18,7 @@
 WINDOWS = STEPS // WINDOW
 SLOTS = 16
 
-CUT = 408
-VLIM = 32 << 20
+CUTS = (424, 352)
 
 LOSS = 0.0045
 WARMUP = 50.0
@@ -74,45 +73,13 @@
     return high, (value - high.astype(jnp.float32)).astype(jnp.bfloat16)
 
 
-def gather_kernel(
-    coef_hbm, sky_hbm, hour_hbm, out_ref,
-    coef_raw, sky_raw, hour_raw, coef_own, coef_sib, coef_x, coef_high, coef_low, sky_buf, sky_high, sky_low, prod,
-    load_sem, sky_sems, sky_send, coef_sems, coef_send, prod_send, prod_recv, prod_own,
+def exchange(
+    place, load_sem, out_ref, coef_raw, coef_own, coef_sib, coef_x, coef_high, coef_low, sky_buf, sky_high, sky_low, prod,
+    sky_sems, sky_send, coef_sems, coef_send, prod_send, prod_recv, prod_own, coef_hbm,
 ):
-    place = coordinates()
-    x, y, z, c = place
-    h, s = device(place)
-    me = h * 16 + s
-    loads = [
-        pltpu.make_async_copy(sky_hbm, sky_raw, load_sem.at[0]),
-        pltpu.make_async_copy(hour_hbm.at[pl.ds(pl.multiple_of((me // 4) * 8, 8), 8)], hour_raw, load_sem.at[1]),
-        pltpu.make_async_copy(coef_hbm, coef_raw, load_sem.at[2]),
-    ]
-    for load in loads:
-        load.start()
-
-    partners = [along_second(place, 1), along_second(place, 3), sibling(place)]
-    for k in (1, 2, 3):
-        for partner in (along_third(place, k), along_first(place, k)):
-            partners += [partner, sibling(partner)]
-    barrier = pltpu.get_barrier_semaphore()
-    for partner in partners:
-        pl.semaphore_signal(barrier, inc=1, device_id=device(partner), device_id_type=MESH)
-
-    loads[0].wait()
-    loads[1].wait()
-    sky_parts = two_parts(sky_raw[...])
-    sky_buf[0, pl.ds(PATCHES - 1, 8), :] = jnp.zeros((8, 256), jnp.float32)
-    for half in range(2):
-        column = hour_raw[pl.ds((me % 4) * 2 + half, 1), :] - me * 256
-        chosen = (lax.broadcasted_iota(jnp.int32, (256, 128), 0) == column).astype(jnp.bfloat16)
-        ordered = sum(jnp.dot(part, chosen, preferred_element_type=jnp.float32) for part in sky_parts)
-        sky_buf[0, pl.ds(0, PATCHES), pl.ds(half * 128, 128)] = ordered
-    sky_high[pl.ds(576, 64), :] = jnp.zeros((64, 256), jnp.bfloat16)
-    sky_low[pl.ds(576, 64), :] = jnp.zeros((64, 256), jnp.bfloat16)
-    pl.semaphore_wait(barrier, len(partners))
-
-    rows_of = ((0, CUT), (CUT, ROWS))
+    core = place[3]
+    cut = CUTS[core]
+    rows_of = ((0, cut), (cut, ROWS))
 
     def send_sky(part, i, j, second, by, which=None):
         start, stop = rows_of[part]
@@ -140,14 +107,14 @@
             rows = sky_buf.at[slot, pl.ds(start, stop - start)]
             pltpu.make_async_copy(rows, rows, sky_sems.at[part, slot, which]).wait()
 
-        if across == 2 or (across == 0 and along == 2):
-            wait(0, start, middle(start, stop))
-            wait(1, middle(start, stop), stop)
-        elif (part, i) == (0, 0):
+        if across == 2 or (across == 0 and along == 2) or (part, i) == (0, 0):
             wait(0, start, middle(start, stop))
             wait(1, middle(start, stop), stop)
         else:
             wait(0, start, stop)
+
+    def forward_sky(part, i, j):
+        along, across = (i, j) if part == 0 else (j, i)
         inner, outer = part == 1, part == 0
         if across == 0:
             if along == 3:
@@ -165,7 +132,7 @@
         send_sky(part, 0, 0, second, 1, which)
         send_sky(part, 0, 0, second, -1, which)
 
-    loads[2].wait()
+    pltpu.make_async_copy(coef_hbm, coef_raw, load_sem).wait()
     coef_own[:, pl.ds(512, 128)] = jnp.zeros((512, 128), jnp.float32)
     for tile in range(4):
         lanes = pl.ds(tile * 128, 128)
@@ -187,7 +154,8 @@
         coef_high[rows, :] = high
         coef_low[rows, :] = low
 
-    def x_copies(source, other):
+    def x_copies(other):
+        source = (coef_own, coef_sib)[other]
         return [
             coef_copy(source.at[row_of(place)], coef_x.at[n, other], 1 + n * 2 + other, along_x(place, by))
             for n, by in ((0, 3), (1, 1))
@@ -195,50 +163,18 @@
 
     to_sibling = coef_copy(coef_own, coef_sib, 0, sibling(place))
     to_sibling.start()
-
-    @pl.when(c == 1)
-    def _():
-        for copy in x_copies(coef_own, 0):
+    if core == 1:
+        for copy in x_copies(0):
             copy.start()
-
-    for k in (0, 2):
+    here = (0, 1, 2, 3) if core == 0 else (0, 2)
+    for k in here:
         put_coef(k, 0, coef_own[row_of(along_third(place, k)), :])
-
-    @pl.when(c == 0)
-    def _():
-        for k in (1, 3):
-            put_coef(k, 0, coef_own[row_of(along_third(place, k)), :])
-
     to_sibling.wait()
-
-    @pl.when(c == 1)
-    def _():
-        for copy in x_copies(coef_sib, 1):
+    if core == 1:
+        for copy in x_copies(1):
             copy.start()
-
-    for k in (0, 2):
+    for k in here:
         put_coef(k, 1, coef_sib[row_of(along_third(place, k)), :])
-
-    @pl.when(c == 0)
-    def _():
-        for k in (1, 3):
-            put_coef(k, 1, coef_sib[row_of(along_third(place, k)), :])
-
-    def await_all(*parts):
-        for part, i, j in parts:
-            await_sky(part, i, j)
-
-    await_all((1, 0, 3), (1, 0, 1))
-    send_sky(0, 0, 0, True, 1, 1)
-    send_sky(0, 0, 0, True, -1, 1)
-    await_all((0, 3, 0), (0, 1, 0), (1, 3, 0), (1, 1, 0))
-
-    @pl.when(c == 1)
-    def _():
-        for other in range(2):
-            for n, copy in enumerate(x_copies((coef_own, coef_sib)[other], other)):
-                copy.wait()
-                put_coef(2 * n + 1, other, coef_x[n, other])
 
     def multiply(i, j):
         slot = slot_of(i, j)
@@ -278,25 +214,86 @@
                     device_id_type=MESH,
                 ).start()
 
-    def multiply_all(*chunks):
-        for i, j in chunks:
-            multiply(i, j)
-
-    multiply_all((0, 0), (3, 0), (1, 0))
-    await_all((1, 0, 2), (1, 3, 3), (1, 3, 1), (1, 1, 3), (1, 1, 1), (0, 2, 0), (1, 2, 0))
-    multiply_all((2, 0))
-    await_all((0, 0, 3), (0, 0, 1))
-    multiply_all((0, 3), (0, 1))
-    await_all((1, 3, 2), (1, 1, 2))
-    await_all((0, 3, 3), (0, 3, 1))
-    multiply_all((3, 3), (3, 1))
-    await_all((0, 1, 3), (0, 1, 1))
-    multiply_all((1, 3), (1, 1))
-    await_all((1, 2, 3), (1, 2, 1), (1, 2, 2), (0, 2, 3), (0, 2, 1))
-    multiply_all((2, 3), (2, 1))
-    for i in (0, 3, 1, 2):
-        await_all((0, i, 2))
-        multiply_all((i, 2))
+    def run(*steps):
+        for step in steps:
+            do, *at = step
+            if do == "coef":
+                for other in range(2):
+                    for n, copy in enumerate(x_copies(other)):
+                        copy.wait()
+                        put_coef(2 * n + 1, other, coef_x[n, other])
+            elif do == "own":
+                send_sky(0, 0, 0, True, 1, 1)
+                send_sky(0, 0, 0, True, -1, 1)
+            elif do == "mul":
+                for i, j in at:
+                    multiply(i, j)
+            else:
+                part = int(do[0])
+                for i, j in at:
+                    if "f" not in do:
+                        await_sky(part, i, j)
+                    if "w" not in do:
+                        forward_sky(part, i, j)
+
+    near = (
+        ("1", (0, 3), (0, 1)),
+        ("own",),
+        ("0", (3, 0), (1, 0)),
+        ("1", (3, 0), (1, 0)),
+    )
+    sides = ("1", (3, 3), (3, 1), (1, 3), (1, 1))
+    far = (
+        ("0", (1, 3), (1, 1)),
+        ("mul", (1, 3), (1, 1)),
+        ("1", (2, 3), (2, 1), (2, 2)),
+        ("0", (2, 3), (2, 1)),
+        ("mul", (2, 3), (2, 1)),
+        ("0", (0, 2)),
+        ("mul", (0, 2)),
+        ("0", (3, 2)),
+        ("mul", (3, 2)),
+        ("0", (1, 2)),
+        ("mul", (1, 2)),
+        ("0", (2, 2)),
+        ("mul", (2, 2)),
+    )
+    if core == 0:
+        run(
+            ("mul", (0, 0)),
+            *near,
+            ("mul", (3, 0), (1, 0)),
+            ("1", (0, 2)),
+            ("0w", (0, 3), (0, 1)),
+            ("mul", (0, 3), (0, 1)),
+            sides,
+            ("0w", (3, 3), (3, 1)),
+            ("mul", (3, 3), (3, 1)),
+            ("0", (2, 0)),
+            ("0f", (0, 3), (0, 1), (3, 3), (3, 1)),
+            ("1", (2, 0)),
+            ("mul", (2, 0)),
+            ("1", (3, 2), (1, 2)),
+            *far,
+        )
+    else:
+        run(
+            *near,
+            ("coef",),
+            ("mul", (0, 0), (3, 0), (1, 0)),
+            ("1", (0, 2)),
+            sides,
+            ("0w", (0, 3), (0, 1)),
+            ("mul", (0, 3), (0, 1)),
+            ("0", (2, 0)),
+            ("0f", (0, 3), (0, 1)),
+            ("1", (2, 0)),
+            ("mul", (2, 0)),
+            ("0", (3, 3), (3, 1)),
+            ("mul", (3, 3), (3, 1)),
+            ("1", (3, 2), (1, 2)),
+            *far,
+        )
 
     def finish(ref, sem):
         pltpu.make_async_copy(ref, ref, sem).wait()
@@ -305,6 +302,53 @@
     finish(prod.at[pl.ds(0, 14)], prod_send)
     finish(prod.at[pl.ds(0, 2)], prod_own)
     finish(out_ref.at[pl.ds(0, WINDOWS // 8 * 7)], prod_recv)
+
+def gather_kernel(
+    coef_hbm, sky_hbm, hour_hbm, out_ref,
+    coef_raw, sky_raw, hour_raw, coef_own, coef_sib, coef_x, coef_high, coef_low, sky_buf, sky_high, sky_low, prod,
+    load_sem, sky_sems, sky_send, coef_sems, coef_send, prod_send, prod_recv, prod_own,
+):
+    place = coordinates()
+    h, s = device(place)
+    me = h * 16 + s
+    loads = [
+        pltpu.make_async_copy(sky_hbm, sky_raw, load_sem.at[0]),
+        pltpu.make_async_copy(hour_hbm.at[pl.ds(pl.multiple_of((me // 4) * 8, 8), 8)], hour_raw, load_sem.at[1]),
+        pltpu.make_async_copy(coef_hbm, coef_raw, load_sem.at[2]),
+    ]
+    for load in loads:
+        load.start()
+
+    partners = [along_second(place, 1), along_second(place, 3), sibling(place)]
+    for k in (1, 2, 3):
+        for partner in (along_third(place, k), along_first(place, k)):
+            partners += [partner, sibling(partner)]
+    barrier = pltpu.get_barrier_semaphore()
+    for partner in partners:
+        pl.semaphore_signal(barrier, inc=1, device_id=device(partner), device_id_type=MESH)
+
+    loads[0].wait()
+    loads[1].wait()
+    sky_parts = two_parts(sky_raw[...])
+    sky_buf[0, pl.ds(PATCHES - 1, 8), :] = jnp.zeros((8, 256), jnp.float32)
+    for half in range(2):
+        column = hour_raw[pl.ds((me % 4) * 2 + half, 1), :] - me * 256
+        chosen = (lax.broadcasted_iota(jnp.int32, (256, 128), 0) == column).astype(jnp.bfloat16)
+        ordered = sum(jnp.dot(part, chosen, preferred_element_type=jnp.float32) for part in sky_parts)
+        sky_buf[0, pl.ds(0, PATCHES), pl.ds(half * 128, 128)] = ordered
+    sky_high[pl.ds(576, 64), :] = jnp.zeros((64, 256), jnp.bfloat16)
+    sky_low[pl.ds(576, 64), :] = jnp.zeros((64, 256), jnp.bfloat16)
+    pl.semaphore_wait(barrier, len(partners))
+
+
+    for core in range(2):
+        @pl.when(place[3] == core)
+        def _(core=core):
+            exchange(
+                (*place[:3], core), load_sem.at[2], out_ref, coef_raw, coef_own, coef_sib, coef_x, coef_high, coef_low,
+                sky_buf, sky_high, sky_low, prod, sky_sems, sky_send, coef_sems, coef_send, prod_send, prod_recv, prod_own, coef_hbm,
+            )
+
 
 def irradiance(coefficients, sky, hours):
     coefficients, sky, hours = [pltpu.with_memory_space_constraint(a, pltpu.HBM) for a in (coefficients, sky, hours)]
@@ -338,68 +382,75 @@
             dma,
         ],
         compiler_params=pltpu.CompilerParams(
-            collective_id=0, has_side_effects=True, vmem_limit_bytes=VLIM
+            collective_id=0, has_side_effects=True, vmem_limit_bytes=32 << 20
         ),
         name="irradiance",
     )(coefficients, sky, hours)
 
 
-GROUP = 64
-
-
-def thermal_kernel(flux_ref, air_ref, module_ref, out_ref, means):
+GROUP = 32
+BUFFERS = 4
+
+
+def thermal_kernel(flux_ref, air_ref, module_ref, out_hbm, means, buffers, sems):
     f32, bf16 = jnp.float32, jnp.bfloat16
-
-    @pl.when(pl.program_id(0) == 0)
-    def _():
-        means[pl.ds(0, MODS), :] = jnp.zeros((MODS, WINDOW), f32)
-
-    @pl.when(pl.program_id(0) > 0)
-    def _():
-        means[pl.ds(0, MODS), :] = means[pl.ds(GROUP * MODS, MODS), :]
-
-    member = lax.broadcasted_iota(jnp.int32, (MODS, POINTS), 0) == module_ref[...]
-    onehot = member.astype(bf16)
+    onehot = (lax.broadcasted_iota(jnp.int32, (MODS, POINTS), 0) == module_ref[...]).astype(bf16)
     both = jnp.concatenate([onehot, onehot], axis=1)
-    for w in range(GROUP):
-        stacked = jnp.concatenate(two_parts(flux_ref[w]), axis=0)
-        mean = jnp.dot(both, stacked, preferred_element_type=f32) / (POINTS // MODS)
-        means[pl.ds((w + 1) * MODS, MODS), :] = mean
+    none = jnp.zeros_like(both)
+    pair = jnp.concatenate([jnp.concatenate([both, none], axis=1), jnp.concatenate([none, both], axis=1)], axis=0)
     row = lax.broadcasted_iota(jnp.int32, (WINDOW, WINDOW), 0)
     col = lax.broadcasted_iota(jnp.int32, (WINDOW, WINDOW), 1)
-    upper, lower = (row <= col).astype(bf16), (row > col).astype(bf16)
-    heat = jnp.zeros((GROUP * MODS, WINDOW), f32)
-    for first, weights in ((MODS, upper), (0, lower)):
-        for part in two_parts(means[pl.ds(first, GROUP * MODS), :]):
-            heat = heat + jnp.dot(part, weights, preferred_element_type=f32)
-    heat = heat / WINDOW
+    summing = jnp.concatenate([(row <= col).astype(bf16), (row > col).astype(bf16)], axis=0)
     name = lax.broadcasted_iota(jnp.int32, (MODS, WINDOW), 0).astype(bf16)
     index = lax.dot_general(onehot, name, (((0,), (0,)), ((), ())), preferred_element_type=f32)
     index = index.astype(jnp.int32)
-    for w in range(GROUP):
-        warmth = air_ref[pl.ds(w, 1), :] + WARMUP * heat[w * MODS : (w + 1) * MODS, :]
-        scale = 1.0 - LOSS * (warmth - NOMINAL)
-        for r in range(POINTS // 8):
-            spread = jnp.take_along_axis(scale, index[r * 8 : (r + 1) * 8, :], axis=0)
-            rows = pl.ds(r * 8, 8)
-            out_ref[rows, pl.ds(w * WINDOW, WINDOW)] = flux_ref[w, rows, :] * spread
+    means[pl.ds(0, MODS), :] = jnp.zeros((MODS, WINDOW), f32)
+
+    def copy(group):
+        slot = group % BUFFERS
+        columns = pl.ds(group * GROUP * WINDOW, GROUP * WINDOW)
+        return pltpu.make_async_copy(buffers.at[slot], out_hbm.at[:, columns], sems.at[slot])
+
+    groups = WINDOWS // GROUP
+    for group in range(groups):
+        if group >= BUFFERS:
+            copy(group - BUFFERS).wait()
+        start = group * GROUP
+        for w in range(start, start + GROUP, 2):
+            parts = jnp.concatenate([*two_parts(flux_ref[w]), *two_parts(flux_ref[w + 1])], axis=0)
+            mean = jnp.dot(pair, parts, preferred_element_type=f32) / (POINTS // MODS)
+            means[pl.ds((w + 1) * MODS, 2 * MODS), :] = mean
+        now = two_parts(means[pl.ds((start + 1) * MODS, GROUP * MODS), :])
+        before = two_parts(means[pl.ds(start * MODS, GROUP * MODS), :])
+        heat = jnp.zeros((GROUP * MODS, WINDOW), f32)
+        for part in range(2):
+            windows = jnp.concatenate([now[part], before[part]], axis=1)
+            heat = heat + jnp.dot(windows, summing, preferred_element_type=f32)
+        heat = heat / WINDOW
+        for w in range(GROUP):
+            warmth = air_ref[pl.ds(start + w, 1), :] + WARMUP * heat[w * MODS : (w + 1) * MODS, :]
+            scale = 1.0 - LOSS * (warmth - NOMINAL)
+            for r in range(POINTS // 8):
+                rows = pl.ds(r * 8, 8)
+                spread = jnp.take_along_axis(scale, index[r * 8 : (r + 1) * 8, :], axis=0)
+                buffers[group % BUFFERS, rows, pl.ds(w * WINDOW, WINDOW)] = flux_ref[start + w, rows, :] * spread
+        copy(group).start()
+    for group in range(groups - BUFFERS, groups):
+        copy(group).wait()
 
 
 def thermal_power(flux, air, modules):
     return pl.pallas_call(
         thermal_kernel,
-        grid=(WINDOWS // GROUP,),
         out_shape=jax.ShapeDtypeStruct((POINTS, STEPS), jnp.float32),
-        in_specs=[
-            pl.BlockSpec((GROUP, POINTS, WINDOW), lambda g: (g, 0, 0)),
-            pl.BlockSpec((GROUP, WINDOW), lambda g: (g, 0)),
-            pl.BlockSpec((1, POINTS), lambda g: (0, 0)),
+        in_specs=[pl.BlockSpec(memory_space=pltpu.VMEM)] * 3,
+        out_specs=pl.BlockSpec(memory_space=pl.ANY),
+        scratch_shapes=[
+            pltpu.VMEM(((WINDOWS + 1) * MODS, WINDOW), jnp.float32),
+            pltpu.VMEM((BUFFERS, POINTS, GROUP * WINDOW), jnp.float32),
+            pltpu.SemaphoreType.DMA((BUFFERS,)),
         ],
-        out_specs=pl.BlockSpec((POINTS, GROUP * WINDOW), lambda g: (0, g)),
-        scratch_shapes=[
-            pltpu.VMEM(((GROUP + 1) * MODS, WINDOW), jnp.float32),
-        ],
-        compiler_params=pltpu.CompilerParams(vmem_limit_bytes=16 << 20),
+        compiler_params=pltpu.CompilerParams(vmem_limit_bytes=24 << 20),
         name="thermal",
     )(flux, air, modules)
 

time: 86.1 us -> 80.7 us (0.937)
  Pallas kernels: 85.9 us -> 80.3 us
    pallas_call x1, Pallas kernels: 79.5 us -> 76.1 us  [irradiance(): pl.pallas_call(gather_kernel, out_shape=jax.ShapeDtypeStruct((WINDOWS, PO...]
    pallas_call x1, Pallas kernels: 6.44 us -> 4.23 us  [thermal_power(): pl.pallas_call(thermal_kernel, out_shape=jax.ShapeDtypeStruct((POINTS, ST...]
where the time goes in v3:
time: 80.7 us; the launch traced here: 80.5 us
  Pallas kernels  80.3 us (100%)
    pallas_call x1, Pallas kernels, irradiance(): pl.pallas_call(gather_kernel, out_shape=jax.ShapeDtypeStruct((WINDOWS, PO...  76.1 us
    pallas_call x1, Pallas kernels, thermal_power(): pl.pallas_call(thermal_kernel, out_shape=jax.ShapeDtypeStruct((POINTS, ST...  4.23 us

profile of v3, /device:TPU:1, one launch (start us, length us, event | category | flops | bytes accessed | tf_op | source)
XLA Modules:
  0.0 80.5 jit_solution(11045638145244544110)
XLA Ops:
  0.0 0.0 copy-start.1
  0.0 0.0 copy-start
  0.0 76.1 %irradiance.1.flux_ref = f32[256,64,128]{2,1,0:T(8,128)S(1)} custom-call(f32[577,1,512]{2,1,0:T(1,128)} %coef_hbm.1, f32[577,256]{1,0:T(8,128)} %sky_hbm.1, s32[256,128]{1,0:T(8,128)} %bitcast.6), custom_call_target="tpu_custom_call" | custom-call | tf_op jit(solution)/shard_map/irradiance/pallas_call | solution.py:357
  76.1 0.0 copy-done.1
  76.1 0.0 copy-done
  76.1 4.2 %thermal.1 = f32[64,32768]{1,0:T(8,128)} custom-call(f32[256,64,128]{2,1,0:T(8,128)S(1)} %irradiance.1.flux_ref, f32[256,128]{1,0:T(8,128)S(1)} %bitcast.4, s32[1,64]{1,0:T(1,128)S(1)} %bitcast.5), custom_call_target="tpu_custom_call" | custom-call | tf_op jit(solution)/shard_map/thermal/pallas_call | solution.py:443
Async XLA Ops:
  0.0 76.1 %copy-start.1 = (s32[1,1,64]{2,1,0:T(1,128)S(1)}, s32[1,1,64]{2,1,0:T(1,128)}, u32[]{:S(2)}) copy-start(s32[1,1,64]{2,1,0:T(1,128)} %param.9) | copy-start | bytes 772
  0.0 76.1 %copy-start = (f32[32768]{0:T(1024)S(1)}, f32[32768]{0:T(1024)}, u32[]{:S(2)}) copy-start(f32[32768]{0:T(1024)} %param.7) | copy-start | bytes 393220

commit v4 on v3

v4 whole, which is shorter than its diff:
```python
import functools

import jax
import jax.numpy as jnp
from jax import lax
from jax.experimental import pallas as pl
from jax.experimental.pallas import tpu as pltpu
from jax.sharding import PartitionSpec as P

MESH = pl.DeviceIdType.MESH
PATCHES = 577
ROWS = 584
DEPTH = 640
POINTS = 64
MODS = 8
WINDOW = 128
STEPS = 32768
WINDOWS = STEPS // WINDOW
SLOTS = 16

X0, X1, Y0, Y1, Z0, Z1 = range(6)
SIDES = ((Z0, Z1, X0), (X1, Y0, Y1))
PIECES = ((0, 200), (200, 392), (392, 584))


def bits(*dimensions):
    return sum(1 << d for d in dimensions)


class Plan:
    def __init__(self, core):
        self.bridge, self.cube = SIDES[core], SIDES[1 - core]
        self.far = bits(*self.bridge)
        near = [bits(*(d for n, d in enumerate(self.cube) if at >> n & 1)) for at in range(8)]
        self.nodes = near + [self.far | node for node in near]
        self.trees = [self.tree_of(piece) for piece in range(3)]
        self.relays = [node for tree in self.trees for node, _, _ in tree[:2]]

    def orders(self, piece):
        return self.cube[piece:] + self.cube[:piece], self.bridge[piece:] + self.bridge[:piece]

    def tree_of(self, piece):
        (a, b, c), (p, q, r) = self.orders(piece)
        tree = [(bits(p), 0, p), (bits(p, q), bits(p), q), (self.far, bits(p, q), r)]
        for far in (0, self.far):
            for node, parent, d in (
                (bits(a), 0, a), (bits(b), 0, b), (bits(c), 0, c), (bits(a, b), bits(a), b), (bits(a, c), bits(a), c),
                (bits(b, c), bits(b), c), (bits(a, b, c), bits(a, b), c),
            ):
                tree.append((far | node, far | parent, d))
        return tree


LOSS = 0.0045
WARMUP = 50.0
NOMINAL = 25.0


def coordinates():
    h, s = lax.axis_index("hours"), lax.axis_index("sensor")
    return (h // 4) * 2 + s // 8, (s // 2) % 4, h % 4, s % 2


def flipped(place, dimension):
    moved = list(place)
    at = moved[dimension // 2]
    moved[dimension // 2] = 3 - at if dimension % 2 else at + 1 - 2 * (at % 2)
    return tuple(moved)


def node_of(place, node):
    for dimension in range(6):
        if node >> dimension & 1:
            place = flipped(place, dimension)
    return place


def sibling(place):
    x, y, z, c = place
    return x, y, z, 1 - c


def device(place):
    x, y, z, c = place
    return (x // 2) * 4 + z, ((x % 2) * 4 + y) * 2 + c


def two_parts(value):
    high = value.astype(jnp.bfloat16)
    return high, (value - high.astype(jnp.float32)).astype(jnp.bfloat16)


def exchange(
    place, load_sem, out_ref, coef_raw, coef_own, coef_sib, coef_next, coef_high, coef_low, sky_buf, relay, sky_high, sky_low, prod,
    sky_sems, sky_send, coef_sems, coef_send, prod_send, prod_recv, prod_own, coef_hbm,
):
    core = place[3]
    plan = Plan(core)
    nodes, relays, far, orders = plan.nodes, plan.relays, plan.far, plan.orders

    def chunk(node, piece):
        start, stop = PIECES[piece]
        if node in nodes:
            return sky_buf.at[nodes.index(node), pl.ds(start, stop - start)]
        return relay.at[relays.index(node), pl.ds(0, stop - start)]

    def sem_of(node, piece):
        return sky_sems.at[(nodes + relays).index(node), piece]

    def forward_sky(node, piece, among=range(6)):
        for to, parent, dimension in plan.trees[piece]:
            if parent == node and dimension in among:
                pltpu.make_async_remote_copy(
                    src_ref=chunk(node, piece),
                    dst_ref=chunk(to, piece),
                    send_sem=sky_send.at[int(to & far == far)],
                    recv_sem=sem_of(to, piece),
                    device_id=device(flipped(place, dimension)),
                    device_id_type=MESH,
                ).start()

    def await_sky(node, piece):
        rows = chunk(node, piece)
        pltpu.make_async_copy(rows, rows, sem_of(node, piece)).wait()

    def spread_sky(node, rounds=(0, 1, 2)):
        for n in rounds:
            for piece in range(3):
                forward_sky(node, piece, orders(piece)[0][n : n + 1])

    for piece in range(3):
        forward_sky(0, piece, plan.bridge)
    spread_sky(0, (0,))

    pltpu.make_async_copy(coef_hbm, coef_raw, load_sem).wait()
    coef_own[:, pl.ds(512, 128)] = jnp.zeros((512, 128), jnp.float32)
    for tile in range(4):
        lanes = pl.ds(tile * 128, 128)
        whole = coef_raw[:, 0, lanes]
        coef_own[lanes, pl.ds(0, PATCHES)] = whole.T

    def coef_copy(src, dst, sem, to, other):
        return pltpu.make_async_remote_copy(
            src_ref=src, dst_ref=dst, send_sem=coef_send.at[sem], recv_sem=coef_sems.at[sem, other],
            device_id=device(to), device_id_type=MESH,
        )

    def row_of(place):
        return pl.ds(pl.multiple_of(device(place)[0] * 64, 64), 64)

    def put_coef(block, other, value):
        high, low = two_parts(value)
        rows = pl.ds(block * 128 + other * 64, 64)
        coef_high[rows, :] = high
        coef_low[rows, :] = low

    own = coef_own.at[row_of(place)]

    def next_copy(dimension):
        to = flipped(place, dimension)
        server = 0 if dimension in SIDES[0] else 1
        return coef_copy(own, coef_next.at[SIDES[server].index(dimension), core], dimension, (*to[:3], server), core)

    sent = [next_copy(dimension) for dimension in (X0, X1, Y0, Y1)]
    for copy in sent:
        copy.start()
    spread_sky(0, (1, 2))
    local = [place] if core == 0 else [place, flipped(place, Z0), flipped(place, Z1)]
    to_sibling = [
        coef_copy(coef_own.at[row_of(at)], coef_sib.at[block], 4 + block, sibling(place), 0) for block, at in enumerate(local)
    ]
    for copy in to_sibling:
        copy.start()
    here = (place, flipped(place, Z0), flipped(place, Z1)) if core == 0 else (place,)
    for block, at in enumerate(here):
        put_coef(block, 0, coef_own[row_of(at), :])
    for copy in to_sibling:
        copy.wait_send()
    for block in range(len(here)):
        pltpu.make_async_copy(coef_sib.at[block], coef_sib.at[block], coef_sems.at[4 + block, 0]).wait()
        put_coef(block, 1, coef_sib[block])

    def multiply(node):
        slot = nodes.index(node)
        high, low = two_parts(sky_buf[slot, pl.ds(0, 576), :])
        sky_high[pl.ds(0, 576), :] = high
        sky_low[pl.ds(0, 576), :] = low
        high, low = two_parts(sky_buf[slot, pl.ds(576, 8), :])
        pad = jnp.zeros((8, 256), jnp.bfloat16)
        sky_high[pl.ds(576, 16), :] = jnp.concatenate([high, pad], axis=0)
        sky_low[pl.ds(576, 16), :] = jnp.concatenate([low, pad], axis=0)

        @pl.loop(0, 2)
        def _(tile):
            rows = pl.ds(pl.multiple_of(tile * 256, 256), 256)
            both = (
                jnp.dot(coef_high[rows, :], sky_low[...], preferred_element_type=jnp.float32)
                + jnp.dot(coef_low[rows, :], sky_high[...], preferred_element_type=jnp.float32)
            ) + jnp.dot(coef_high[rows, :], sky_high[...], preferred_element_type=jnp.float32)
            for half in range(2):
                prod[slot, half, rows, :] = both[:, half * 128 : (half + 1) * 128]

        owner_h, owner_s = device(node_of(place, node))
        windows = pl.ds((owner_h * 16 + owner_s) * 2, 2)
        for block in (3, 1, 2, 0):
            to = flipped(place, plan.bridge[block - 1]) if block else place
            for other in range(2):
                source = prod.at[slot, :, pl.ds(block * 128 + other * 64, 64)]
                if (block, other) == (0, 0):
                    pltpu.make_async_copy(source, out_ref.at[windows], prod_own).start()
                    continue
                pltpu.make_async_remote_copy(
                    src_ref=source,
                    dst_ref=out_ref.at[windows],
                    send_sem=prod_send,
                    recv_sem=prod_recv,
                    device_id=device(sibling(to) if other else to),
                    device_id_type=MESH,
                ).start()

    def take(pick):
        for piece in range(3):
            node = pick(*orders(piece))
            await_sky(node, piece)
            if node != far:
                forward_sky(node, piece)

    def multiply_all(*nodes):
        for node in nodes:
            multiply(node)

    a, b, c = plan.cube
    singles = (bits(a), bits(b), bits(c))
    doubles = (bits(a, b), bits(b, c), bits(a, c))
    take(lambda cube, bridge: bits(bridge[0]))
    take(lambda cube, bridge: bits(cube[0]))
    for copy in sent:
        copy.wait_send()
    for n, dimension in enumerate(plan.bridge):
        if dimension in (Z0, Z1):
            continue
        for other in range(2):
            came = coef_next.at[n, core if other == 0 else 1 - core]
            sem = core if other == 0 else 1 - core
            pltpu.make_async_copy(came, came, coef_sems.at[dimension, sem]).wait()
            put_coef(1 + n, other, came[...])
    take(lambda cube, bridge: bits(bridge[0], bridge[1]))
    multiply_all(0)
    take(lambda cube, bridge: bits(cube[1]))
    take(lambda cube, bridge: bits(cube[2]))
    take(lambda cube, bridge: far)
    spread_sky(far)
    multiply_all(*singles)
    take(lambda cube, bridge: bits(cube[0], cube[1]))
    multiply_all(far)
    take(lambda cube, bridge: bits(cube[0], cube[2]))
    take(lambda cube, bridge: bits(cube[1], cube[2]))
    take(lambda cube, bridge: far | bits(cube[0]))
    multiply_all(*doubles)
    take(lambda cube, bridge: bits(*cube))
    take(lambda cube, bridge: far | bits(cube[1]))
    multiply_all(bits(*plan.cube))
    take(lambda cube, bridge: far | bits(cube[2]))
    multiply_all(*(far | node for node in singles))
    take(lambda cube, bridge: far | bits(cube[0], cube[1]))
    take(lambda cube, bridge: far | bits(cube[0], cube[2]))
    take(lambda cube, bridge: far | bits(cube[1], cube[2]))
    multiply_all(*(far | node for node in doubles))
    take(lambda cube, bridge: far | bits(*cube))
    multiply_all(far | bits(*plan.cube))

    def finish(ref, sem):
        pltpu.make_async_copy(ref, ref, sem).wait()

    finish(sky_buf.at[pl.ds(0, 9)], sky_send.at[0])
    finish(sky_buf.at[pl.ds(0, 8)], sky_send.at[1])
    finish(prod.at[pl.ds(0, 14)], prod_send)
    finish(prod.at[pl.ds(0, 2)], prod_own)
    finish(out_ref.at[pl.ds(0, WINDOWS // 8 * 7)], prod_recv)


def gather_kernel(
    coef_hbm, sky_hbm, hour_hbm, out_ref,
    coef_raw, sky_raw, hour_raw, coef_own, coef_sib, coef_next, coef_high, coef_low, sky_buf, relay, sky_high, sky_low, prod,
    load_sem, sky_sems, sky_send, coef_sems, coef_send, prod_send, prod_recv, prod_own,
):
    place = coordinates()
    h, s = device(place)
    me = h * 16 + s
    loads = [
        pltpu.make_async_copy(sky_hbm, sky_raw, load_sem.at[0]),
        pltpu.make_async_copy(hour_hbm.at[pl.ds(pl.multiple_of((me // 4) * 8, 8), 8)], hour_raw, load_sem.at[1]),
        pltpu.make_async_copy(coef_hbm, coef_raw, load_sem.at[2]),
    ]
    for load in loads:
        load.start()

    partners = [sibling(place)]
    for dimension in range(6):
        partners += [flipped(place, dimension), sibling(flipped(place, dimension))]
    barrier = pltpu.get_barrier_semaphore()
    for partner in partners:
        pl.semaphore_signal(barrier, inc=1, device_id=device(partner), device_id_type=MESH)

    loads[0].wait()
    loads[1].wait()
    sky_parts = two_parts(sky_raw[...])
    sky_buf[0, pl.ds(PATCHES - 1, 8), :] = jnp.zeros((8, 256), jnp.float32)
    for half in range(2):
        column = hour_raw[pl.ds((me % 4) * 2 + half, 1), :] - me * 256
        chosen = (lax.broadcasted_iota(jnp.int32, (256, 128), 0) == column).astype(jnp.bfloat16)
        ordered = sum(jnp.dot(part, chosen, preferred_element_type=jnp.float32) for part in sky_parts)
        sky_buf[0, pl.ds(0, PATCHES), pl.ds(half * 128, 128)] = ordered
    sky_high[pl.ds(576, 64), :] = jnp.zeros((64, 256), jnp.bfloat16)
    sky_low[pl.ds(576, 64), :] = jnp.zeros((64, 256), jnp.bfloat16)
    pl.semaphore_wait(barrier, len(partners))


    for core in range(2):
        @pl.when(place[3] == core)
        def _(core=core):
            exchange(
                (*place[:3], core), load_sem.at[2], out_ref, coef_raw, coef_own, coef_sib, coef_next, coef_high, coef_low,
                sky_buf, relay, sky_high, sky_low, prod, sky_sems, sky_send, coef_sems, coef_send, prod_send, prod_recv,
                prod_own, coef_hbm,
            )


def irradiance(coefficients, sky, hours):
    coefficients, sky, hours = [pltpu.with_memory_space_constraint(a, pltpu.HBM) for a in (coefficients, sky, hours)]
    f32, bf16 = jnp.float32, jnp.bfloat16
    vmem, dma = pltpu.VMEM, pltpu.SemaphoreType.DMA
    return pl.pallas_call(
        gather_kernel,
        out_shape=jax.ShapeDtypeStruct((WINDOWS, POINTS, WINDOW), f32),
        in_specs=[pl.BlockSpec(memory_space=pltpu.HBM)] * 3,
        out_specs=pl.BlockSpec(memory_space=pl.ANY),
        scratch_shapes=[
            vmem((PATCHES, 1, 512), f32),
            vmem((PATCHES, 256), f32),
            vmem((8, 128), jnp.int32),
            vmem((512, DEPTH), f32),
            vmem((3, 64, DEPTH), f32),
            vmem((3, 2, 64, DEPTH), f32),
            vmem((512, DEPTH), bf16),
            vmem((512, DEPTH), bf16),
            vmem((SLOTS, ROWS, 256), f32),
            vmem((6, 200, 256), f32),
            vmem((DEPTH, 256), bf16),
            vmem((DEPTH, 256), bf16),
            vmem((SLOTS, 2, 512, 128), f32),
            dma((3,)),
            dma((SLOTS + 6, 3)),
            dma((2,)),
            dma((7, 2)),
            dma((7,)),
            dma,
            dma,
            dma,
        ],
        compiler_params=pltpu.CompilerParams(
            collective_id=0, has_side_effects=True, vmem_limit_bytes=32 << 20
        ),
        name="irradiance",
    )(coefficients, sky, hours)


GROUP = 32
BUFFERS = 4


def thermal_kernel(flux_ref, air_ref, module_ref, out_hbm, means, buffers, sems):
    f32, bf16 = jnp.float32, jnp.bfloat16
    onehot = (lax.broadcasted_iota(jnp.int32, (MODS, POINTS), 0) == module_ref[...]).astype(bf16)
    both = jnp.concatenate([onehot, onehot], axis=1)
    none = jnp.zeros_like(both)
    pair = jnp.concatenate([jnp.concatenate([both, none], axis=1), jnp.concatenate([none, both], axis=1)], axis=0)
    row = lax.broadcasted_iota(jnp.int32, (WINDOW, WINDOW), 0)
    col = lax.broadcasted_iota(jnp.int32, (WINDOW, WINDOW), 1)
    summing = jnp.concatenate([(row <= col).astype(bf16), (row > col).astype(bf16)], axis=0)
    name = lax.broadcasted_iota(jnp.int32, (MODS, WINDOW), 0).astype(bf16)
    index = lax.dot_general(onehot, name, (((0,), (0,)), ((), ())), preferred_element_type=f32)
    index = index.astype(jnp.int32)
    means[pl.ds(0, MODS), :] = jnp.zeros((MODS, WINDOW), f32)

    def copy(group):
        slot = group % BUFFERS
        columns = pl.ds(group * GROUP * WINDOW, GROUP * WINDOW)
        return pltpu.make_async_copy(buffers.at[slot], out_hbm.at[:, columns], sems.at[slot])

    groups = WINDOWS // GROUP
    for group in range(groups):
        if group >= BUFFERS:
            copy(group - BUFFERS).wait()
        start = group * GROUP
        for w in range(start, start + GROUP, 2):
            parts = jnp.concatenate([*two_parts(flux_ref[w]), *two_parts(flux_ref[w + 1])], axis=0)
            mean = jnp.dot(pair, parts, preferred_element_type=f32) / (POINTS // MODS)
            means[pl.ds((w + 1) * MODS, 2 * MODS), :] = mean
        now = two_parts(means[pl.ds((start + 1) * MODS, GROUP * MODS), :])
        before = two_parts(means[pl.ds(start * MODS, GROUP * MODS), :])
        heat = jnp.zeros((GROUP * MODS, WINDOW), f32)
        for part in range(2):
            windows = jnp.concatenate([now[part], before[part]], axis=1)
            heat = heat + jnp.dot(windows, summing, preferred_element_type=f32)
        heat = heat / WINDOW
        for w in range(GROUP):
            warmth = air_ref[pl.ds(start + w, 1), :] + WARMUP * heat[w * MODS : (w + 1) * MODS, :]
            scale = 1.0 - LOSS * (warmth - NOMINAL)
            for r in range(POINTS // 8):
                rows = pl.ds(r * 8, 8)
                spread = jnp.take_along_axis(scale, index[r * 8 : (r + 1) * 8, :], axis=0)
                buffers[group % BUFFERS, rows, pl.ds(w * WINDOW, WINDOW)] = flux_ref[start + w, rows, :] * spread
        copy(group).start()
    for group in range(groups - BUFFERS, groups):
        copy(group).wait()


def thermal_power(flux, air, modules):
    return pl.pallas_call(
        thermal_kernel,
        out_shape=jax.ShapeDtypeStruct((POINTS, STEPS), jnp.float32),
        in_specs=[pl.BlockSpec(memory_space=pltpu.VMEM)] * 3,
        out_specs=pl.BlockSpec(memory_space=pl.ANY),
        scratch_shapes=[
            pltpu.VMEM(((WINDOWS + 1) * MODS, WINDOW), jnp.float32),
            pltpu.VMEM((BUFFERS, POINTS, GROUP * WINDOW), jnp.float32),
            pltpu.SemaphoreType.DMA((BUFFERS,)),
        ],
        compiler_params=pltpu.CompilerParams(vmem_limit_bytes=24 << 20),
        name="thermal",
    )(flux, air, modules)


def shards(coefficients, sky, outdoor_air_warmth, hour_column, module_of):
    flux = irradiance(coefficients, sky, hour_column.reshape(WINDOWS, WINDOW))
    power = thermal_power(flux, outdoor_air_warmth.reshape(WINDOWS, WINDOW), module_of.reshape(1, POINTS))
    return power.reshape(1, 1, POINTS, STEPS)


def solution(mesh):
    return jax.shard_map(
        shards,
        mesh=mesh,
        in_specs=(
            P(None, "sensor", None),
            P(None, ("hours", "sensor")),
            P(),
            P(),
            P("sensor", "hours", None),
        ),
        out_specs=P("sensor", "hours", None, None),
        check_vma=False,
    )
```

time: 80.7 us -> 80.2 us (level)
  no operation moved by 1% of the time
where the time goes in v4:
time: 80.2 us; the launch traced here: 80.1 us
  Pallas kernels  79.9 us (100%)
    pallas_call x1, Pallas kernels, irradiance(): pl.pallas_call(gather_kernel, out_shape=jax.ShapeDtypeStruct((WINDOWS, PO...  75.6 us
    pallas_call x1, Pallas kernels, thermal_power(): pl.pallas_call(thermal_kernel, out_shape=jax.ShapeDtypeStruct((POINTS, ST...  4.24 us

profile of v4, /device:TPU:1, one launch (start us, length us, event | category | flops | bytes accessed | tf_op | source)
XLA Modules:
  0.0 80.1 jit_solution(5267964975875308195)
XLA Ops:
  0.0 0.0 copy-start.1
  0.0 0.0 copy-start
  0.0 75.6 %irradiance.1.flux_ref = f32[256,64,128]{2,1,0:T(8,128)S(1)} custom-call(f32[577,1,512]{2,1,0:T(1,128)} %coef_hbm.1, f32[577,256]{1,0:T(8,128)} %sky_hbm.1, s32[256,128]{1,0:T(8,128)} %bitcast.6), custom_call_target="tpu_custom_call" | custom-call | tf_op jit(solution)/shard_map/irradiance/pallas_call | solution.py:333
  75.6 0.0 copy-done.1
  75.6 0.0 copy-done
  75.6 4.2 %thermal.1 = f32[64,32768]{1,0:T(8,128)} custom-call(f32[256,64,128]{2,1,0:T(8,128)S(1)} %irradiance.1.flux_ref, f32[256,128]{1,0:T(8,128)S(1)} %bitcast.4, s32[1,64]{1,0:T(1,128)S(1)} %bitcast.5), custom_call_target="tpu_custom_call" | custom-call | tf_op jit(solution)/shard_map/thermal/pallas_call | solution.py:420
Async XLA Ops:
  0.0 75.6 %copy-start.1 = (s32[1,1,64]{2,1,0:T(1,128)S(1)}, s32[1,1,64]{2,1,0:T(1,128)}, u32[]{:S(2)}) copy-start(s32[1,1,64]{2,1,0:T(1,128)} %param.9) | copy-start | bytes 772
  0.0 75.6 %copy-start = (f32[32768]{0:T(1024)S(1)}, f32[32768]{0:T(1024)}, u32[]{:S(2)}) copy-start(f32[32768]{0:T(1024)} %param.7) | copy-start | bytes 393220

commit v5 on v4

--- a/solution.py
+++ b/solution.py
@@ -366,7 +366,7 @@
 
 
 GROUP = 32
-BUFFERS = 4
+BUFFERS = 8
 
 
 def thermal_kernel(flux_ref, air_ref, module_ref, out_hbm, means, buffers, sems):
@@ -427,7 +427,7 @@
             pltpu.VMEM((BUFFERS, POINTS, GROUP * WINDOW), jnp.float32),
             pltpu.SemaphoreType.DMA((BUFFERS,)),
         ],
-        compiler_params=pltpu.CompilerParams(vmem_limit_bytes=24 << 20),
+        compiler_params=pltpu.CompilerParams(vmem_limit_bytes=28 << 20),
         name="thermal",
     )(flux, air, modules)
 

time: 80.2 us -> 80 us (level)
  no operation moved by 1% of the time
where the time goes in v5:
time: 80 us; the launch traced here: 79.9 us
  Pallas kernels  79.7 us (100%)
    pallas_call x1, Pallas kernels, irradiance(): pl.pallas_call(gather_kernel, out_shape=jax.ShapeDtypeStruct((WINDOWS, PO...  75.6 us
    pallas_call x1, Pallas kernels, thermal_power(): pl.pallas_call(thermal_kernel, out_shape=jax.ShapeDtypeStruct((POINTS, ST...  4.08 us

profile of v5, /device:TPU:1, one launch (start us, length us, event | category | flops | bytes accessed | tf_op | source)
XLA Modules:
  0.0 79.9 jit_solution(8524178912068547855)
XLA Ops:
  0.0 0.0 copy-start.1
  0.0 0.0 copy-start
  0.0 75.6 %irradiance.1.flux_ref = f32[256,64,128]{2,1,0:T(8,128)S(1)} custom-call(f32[577,1,512]{2,1,0:T(1,128)} %coef_hbm.1, f32[577,256]{1,0:T(8,128)} %sky_hbm.1, s32[256,128]{1,0:T(8,128)} %bitcast.6), custom_call_target="tpu_custom_call" | custom-call | tf_op jit(solution)/shard_map/irradiance/pallas_call | solution.py:333
  75.6 0.0 copy-done.1
  75.6 0.0 copy-done
  75.6 4.1 %thermal.1 = f32[64,32768]{1,0:T(8,128)} custom-call(f32[256,64,128]{2,1,0:T(8,128)S(1)} %irradiance.1.flux_ref, f32[256,128]{1,0:T(8,128)S(1)} %bitcast.4, s32[1,64]{1,0:T(1,128)S(1)} %bitcast.5), custom_call_target="tpu_custom_call" | custom-call | tf_op jit(solution)/shard_map/thermal/pallas_call | solution.py:420
Async XLA Ops:
  0.0 75.6 %copy-start.1 = (s32[1,1,64]{2,1,0:T(1,128)S(1)}, s32[1,1,64]{2,1,0:T(1,128)}, u32[]{:S(2)}) copy-start(s32[1,1,64]{2,1,0:T(1,128)} %param.9) | copy-start | bytes 772
  0.0 75.6 %copy-start = (f32[32768]{0:T(1024)S(1)}, f32[32768]{0:T(1024)}, u32[]{:S(2)}) copy-start(f32[32768]{0:T(1024)} %param.7) | copy-start | bytes 393220
